TPU v7x, 128 devices: a whole 4x4x4 slice. The times are simulated.
128 devices in a mesh: row: 8 (over x_lo, z), col: 16 (over x_hi, y, core).
Axes of the slice: x: 4 (x_hi: 2, x_lo: 2; x = x_hi * 2 + x_lo), y: 4, z: 4, core: 2. Of those that a mesh axis runs over, the one named last changes fastest.
Arguments:
- tokens: bfloat16 [2048, 4096], P('row', 'col'), may hold values from -6 to 6
- norm_gain: float32 [4096], replicated, may hold values from 0.1 to 1.9
- expert_ids: int32 [2048, 2], P('row'), may hold values from 0 to 7, all different within a row; in each aligned block of 256 rows (0 to 255, 256 to 511, ...) at most 128 rows name the same one
- gate_weights: float32 [2048, 2], P('row'), may hold values from 0.1 to 1
- w_gate: bfloat16 [8, 4096, 14336], P('row', None, 'col'), may hold values from -0.09375 to 0.09375
- w_up: bfloat16 [8, 4096, 14336], P('row', None, 'col'), may hold values from -0.09375 to 0.09375
- w_down: bfloat16 [8, 14336, 4096], P('row', 'col'), may hold values from -0.046875 to 0.046875
Outputs:
- layer_output: bfloat16 [2048, 4096], P('row', 'col')
Inputs may be any that keep to these rules, and one draw needn't show every extreme that they name: `expert_ids`: the 2 experts of a token differ. In each aligned block of 256 tokens no expert is chosen by more than 128 tokens, a bound that some block reaches.
All inputs are finite; a program needn't handle non-finite values.
Results may differ from a plain program's by a relative error of at most 0.0043.
Values may be sent and summed in bfloat16 or wider, within the bound.
A program may use at most 128 MiB of HBM per device.

v0:
```python
import jax
import jax.numpy as jnp
from jax import lax
from jax.sharding import Mesh
from jax.sharding import PartitionSpec as P

EXPERTS = 8
CAP = 128
COL = ("chip", "core")


def route_tables(expert_ids, expert_count, capacity):
    token_count = expert_ids.shape[0]
    flat_ids = expert_ids.reshape(-1)
    expert_range = jnp.arange(expert_count, dtype=jnp.int32)
    expert_hits = (flat_ids[:, None] == expert_range[None, :]).astype(jnp.int32)
    earlier = jnp.cumsum(expert_hits, axis=0) - expert_hits
    ranks = jnp.sum(earlier * expert_hits, axis=1)
    slot_index = (flat_ids * capacity + ranks).reshape(token_count, -1)
    slot_ids = jnp.arange(expert_count * capacity, dtype=jnp.int32)
    matches = (slot_index[:, :, None] == slot_ids[None, None, :]).astype(jnp.float32)
    picker = jnp.sum(matches, axis=1)
    return (picker.astype(jnp.bfloat16), slot_index)


def combine_rows(slot_rows, slot_index, gate_weights):
    picked = slot_rows[slot_index]
    return jnp.sum(picked * gate_weights[:, :, None], axis=1)


def swap_cores(value):
    return lax.ppermute(value, "core", perm=[(0, 1), (1, 0)])


def body(tokens, norm_gain, expert_ids, gate_weights, w_gate, w_up, w_down):
    chips = lax.psum(1, "chip")
    width = tokens.shape[1]
    core = lax.axis_index("core")
    block = lax.axis_index("chip") * 2 + core
    values = tokens.astype(jnp.float32)
    squares = lax.psum(jnp.sum(values * values, axis=-1, keepdims=True), COL)
    inverse_norm = lax.rsqrt(squares / (width * chips * 2) + 1e-05)
    gain = lax.dynamic_slice_in_dim(norm_gain, block * width, width)
    normed = (values * inverse_norm * gain).astype(jnp.bfloat16)
    picker, slot_index = route_tables(expert_ids, EXPERTS, CAP)
    packed = jnp.einsum("ts,td->sd", picker, normed, preferred_element_type=jnp.float32).astype(
        jnp.bfloat16
    )
    packed = packed.reshape(EXPERTS, CAP, width)
    arrived = lax.all_to_all(packed, "row", split_axis=0, concat_axis=0, tiled=True)
    arrived = arrived.reshape(EXPERTS * CAP, width)
    mine = lax.all_gather(arrived, "chip", axis=0, tiled=False)
    other = swap_cores(mine)
    pair = jnp.where(core == 0, jnp.stack([mine, other], 1), jnp.stack([other, mine], 1))
    slots = arrived.shape[0]
    widened = jnp.transpose(pair, (2, 0, 1, 3)).reshape(slots, chips * 2 * width)
    gate_part = jnp.dot(widened, w_gate[0], preferred_element_type=jnp.float32)
    up_part = jnp.dot(widened, w_up[0], preferred_element_type=jnp.float32)
    hidden = (jax.nn.silu(gate_part) * up_part).astype(jnp.bfloat16)
    outputs = jnp.dot(hidden, w_down[0], preferred_element_type=jnp.float32)
    split = outputs.reshape(slots, chips, 2, width)
    keep = jnp.where(core == 0, split[:, :, 0], split[:, :, 1])
    give = jnp.where(core == 0, split[:, :, 1], split[:, :, 0])
    summed = keep + swap_cores(give)
    shares = lax.psum_scatter(summed, "chip", scatter_dimension=1, tiled=True)
    shares = shares.reshape(EXPERTS, CAP, width)
    returned = lax.all_to_all(shares, "row", split_axis=0, concat_axis=0, tiled=True)
    mixed = combine_rows(returned.reshape(-1, width), slot_index, gate_weights)
    return (tokens.astype(jnp.float32) + mixed).astype(jnp.bfloat16)


def solution(mesh):
    rows, cols = mesh.devices.shape
    split_mesh = Mesh(mesh.devices.reshape(rows, cols // 2, 2), ("row", "chip", "core"))
    placed = (
        P("row", COL),
        P(),
        P("row", None),
        P("row", None),
        P("row", None, COL),
        P("row", None, COL),
        P("row", COL, None),
    )
    return jax.shard_map(
        body, mesh=split_mesh, in_specs=placed, out_specs=P("row", COL), check_vma=False
    )
```

profile of v0, /device:TPU:0, one launch (start us, length us, event | category | flops | bytes accessed | tf_op | source)
XLA Modules:
  0.0 370.8 jit_solution(8695487437753940584)
XLA Ops:
  6.5 0.8 copy.51
  7.4 0.1 eq.48
  7.5 0.1 eq.44
  7.7 1.1 reduce-window.6
  8.8 0.2 slice_reduce_fusion
  9.2 0.1 reduce_sum.39
  9.4 0.7 compare_select_fusion
  10.1 0.3 convert_reduce_fusion
  10.4 1.0 fusion.9
  11.4 38.1 %psum.7 = f32[256,1]{0,1:T(1,128)S(1)} all-reduce(f32[256,1]{0,1:T(1,128)S(1)} %bitcast.67), channel_id=1, replica_groups=mesh['row'=8,'chip'=8,'core'=2] {'chip','core'}, use_global_device_ids=true, to_apply=%region_5.6 | all-reduce | flops 256 | bytes 2048 | tf_op jit(solution)/shard_map/psum | solution.py:41
  49.5 0.8 dynamic_slice.3
  50.3 1.3 convolution_convert_fusion
  51.6 13.9 %all_to_all.10 = bf16[8,128,256]{2,1,0:T(8,128)(2,1)} all-to-all(bf16[8,128,256]{2,1,0:T(8,128)(2,1)S(1)} %bitcast.66), channel_id=1, replica_groups=mesh['row'=8,'chip'=8,'core'=2] {'row'}, dimensions={0} | all-to-all | bytes 1048576 | tf_op jit(solution)/shard_map/all_to_all | solution.py:50
  65.5 67.0 %all-gather.2.cloned.1.call-done = bf16[8,1024,256]{2,1,0:T(8,128)(2,1)} async-done(((bf16[1,1024,256]{2,1,0:T(8,128)(2,1)}), bf16[8,1024,256]{2,1,0:T(8,128)(2,1)}) %all-gather.2.cloned.1.call-update) | async-done | bytes 4194320 | tf_op jit(solution)/shard_map/all_gather | solution.py:52
  132.6 6.4 %copy.54 = bf16[8,1024,256]{1,2,0:T(8,128)(2,1)} copy(bf16[8,1024,256]{2,1,0:T(8,128)(2,1)} %all-gather.2.cloned.1.call-done) | data formatting | bytes 8388608 | tf_op jit(solution)/shard_map/all_gather | solution.py:52
  139.0 10.8 %copy.64 = bf16[4096,896]{1,0:T(8,128)(2,1)} copy(bf16[4096,896]{0,1:T(8,128)(2,1)} %bitcast.60) | data formatting | bytes 14680064 | tf_op jit(solution)/shard_map/dot_general | solution.py:60
  149.8 7.9 %maximum_select_fusion = bf16[8,2,1024,256]{2,3,1,0:T(8,128)(2,1)S(1)} fusion(bf16[8,1,1024,256]{2,3,1,0:T(8,128)(2,1)} %bitcast.7, bf16[8,1,1024,256]{2,3,1,0:T(8,128)(2,1)} %bitcast.57, pred[]{:T(512)S(6)} %eq.43), kind=kLoop, calls=%fused_computation.1 | loop fusion | flops 12582912 | bytes 16777216 | tf_op jit(solution)/shard_map/jit(_where)/select_n | solution.py:54
  157.8 13.0 %fusion.2 = f32[1024,896]{1,0:T(8,128)S(1)} fusion(bf16[1024,4096]{0,1:T(8,128)(2,1)S(1)} %bitcast.58, bf16[1,4096,896]{2,1,0:T(8,128)(2,1)} %param.12), kind=kOutput, calls=%fused_computation.6 | convolution fusion | flops 7516192768 | bytes 19398656 | tf_op jit(solution)/shard_map/dot_general | solution.py:58
  170.9 11.1 %fusion.4 = f32[1024,896]{1,0:T(8,128)} fusion(bf16[1024,4096]{0,1:T(8,128)(2,1)S(1)} %bitcast.59, bf16[1,4096,896]{2,1,0:T(8,128)(2,1)S(1)} %bitcast.70), kind=kOutput, calls=%fused_computation.8 | convolution fusion | flops 7516192768 | bytes 19398656 | tf_op jit(solution)/shard_map/dot_general | solution.py:57
  182.0 13.8 %fusion.6 = f32[1024,8,2,256]{3,0,2,1:T(8,128)} fusion(bf16[8,2,256,896]{3,2,1,0:T(8,128)(2,1)S(1)} %bitcast.63, f32[1024,896]{1,0:T(8,128)S(1)} %fusion.2, f32[1024,896]{1,0:T(8,128)} %fusion.4), kind=kOutput, calls=%fused_computation.13 | convolution fusion | flops 7521697792 | bytes 31457280 | tf_op jit(solution)/shard_map/dot_general | solution.py:60
  195.8 10.1 %select_bitcast_fusion = f32[1024,8,256]{2,0,1:T(8,128)} fusion(f32[1024,8,2,256]{3,0,2,1:T(8,128)} %fusion.6, pred[]{:T(512)S(6)} %eq.43), kind=kLoop, calls=%fused_computation.5 | loop fusion | flops 2097152 | bytes 25165824 | tf_op jit(solution)/shard_map/jit(_where)/select_n | solution.py:63
  205.8 0.5 collective-permute-start.1
  206.3 13.0 %collective-permute-done.1 = f32[1024,8,256]{2,0,1:T(8,128)S(1)} collective-permute-done((f32[1024,8,256]{2,0,1:T(8,128)}, f32[1024,8,256]{2,0,1:T(8,128)S(1)}, u32[]{:S(2)}, u32[]{:S(2)}) %collective-permute-start.1) | collective-permute-done | bytes 8388640 | tf_op jit(solution)/shard_map/ppermute | solution.py:32
  219.3 10.0 %fusion.1 = f32[1024,8,256]{2,0,1:T(8,128)} fusion(f32[1024,8,256]{2,0,1:T(8,128)S(1)} %collective-permute-done.1, f32[1024,8,2,256]{3,0,2,1:T(8,128)} %fusion.6, pred[]{:T(512)S(6)} %eq.43), kind=kLoop, calls=%fused_computation.4 | loop fusion | flops 4194304 | bytes 33554432 | tf_op jit(solution)/shard_map/add | solution.py:64
  229.4 112.7 %reduce-scatter.2.cloned.1.call-done = f32[1024,1,256]{2,0,1:T(8,128)} async-done(((f32[1024,8,256]{2,0,1:T(8,128)}), f32[1024,1,256]{2,0,1:T(8,128)}) %reduce-scatter.2.cloned.1.call-update) | async-done | bytes 1048592 | tf_op jit(solution)/shard_map/reduce_scatter | solution.py:65
  342.1 4.4 %all-to-all-start.1 = ((f32[8,128,256]{2,1,0:T(8,128)}), f32[8,128,256]{2,1,0:T(8,128)S(1)}, u32[]{:S(2)}, u32[]{:S(2)}) async-start(f32[8,128,256]{2,1,0:T(8,128)} %bitcast.65), calls=%async_computation.2 | async-start | bytes 2097152 | tf_op jit(solution)/shard_map/all_to_all | solution.py:67
  346.6 0.1 reshape.53
  347.0 13.7 %all-to-all-done.1 = f32[8,128,256]{2,1,0:T(8,128)S(1)} async-done(((f32[8,128,256]{2,1,0:T(8,128)}), f32[8,128,256]{2,1,0:T(8,128)S(1)}, u32[]{:S(2)}, u32[]{:S(2)}) %all-to-all-start.1) | async-done | bytes 1048608 | tf_op jit(solution)/shard_map/all_to_all | solution.py:67
  360.7 1.6 gather_fusion
  362.3 0.3 reshape.52
  362.6 0.7 multiply_reduce_fusion
  363.3 0.7 fusion.12
  (29 shorter events, 0.6 us)
Async XLA Ops:
  6.5 126.0 %all-gather.2.cloned.1.call-start = ((), (), s32[]{:S(2)}) async-start(), calls=%async_computation.3 | async-start | bytes 4718592 | tf_op jit(solution)/shard_map/all_gather | solution.py:52
  65.5 276.6 %reduce-scatter.2.cloned.1.call-start = ((), (), s32[]{:S(2)}) async-start(), calls=%async_computation.4 | async-start | bytes 9437184 | tf_op jit(solution)/shard_map/reduce_scatter | solution.py:65
  139.0 10.8 %collective-permute-start = (bf16[8,1024,256]{1,2,0:T(8,128)(2,1)}, bf16[8,1024,256]{1,2,0:T(8,128)(2,1)}, u32[]{:S(2)}, u32[]{:S(2)}) collective-permute-start(bf16[8,1024,256]{1,2,0:T(8,128)(2,1)} %copy.54), channel_id=1, source_target_pairs={{0,1},{1,0},{2,3},{3,2},{4,5},{5,4},{6,7},{7,6},{8,9},{9,8},{10,11... | collective-permute-start | bytes 12582920 | tf_op jit(solution)/shard_map/ppermute | solution.py:32
  149.8 21.0 %slice-start.2 = ((s8[7340032]{0:T(1024)(128)(4,1)}), s8[4194304]{0:T(1024)(128)(4,1)S(1)}, s32[]{:S(2)}) async-start(s8[7340032]{0:T(1024)(128)(4,1)} %bitcast.69), calls=%async_computation.7 | async-start | bytes 8388608
  157.8 13.1 %slice-start.3 = ((s8[7340032]{0:T(1024)(128)(4,1)}), s8[3145728]{0:T(1024)(128)(4,1)S(1)}, s32[]{:S(2)}) async-start(s8[7340032]{0:T(1024)(128)(4,1)} %bitcast.69), calls=%async_computation.8 | async-start | bytes 6291456
  157.8 24.2 %slice-start = ((s8[7340032]{0:T(1024)(128)(4,1)}), s8[4194304]{0:T(1024)(128)(4,1)S(1)}, s32[]{:S(2)}) async-start(s8[7340032]{0:T(1024)(128)(4,1)} %bitcast.61), calls=%async_computation.5 | async-start | bytes 8388608
  170.9 11.1 %slice-start.1 = ((s8[7340032]{0:T(1024)(128)(4,1)}), s8[3145728]{0:T(1024)(128)(4,1)S(1)}, s32[]{:S(2)}) async-start(s8[7340032]{0:T(1024)(128)(4,1)} %bitcast.61), calls=%async_computation.6 | async-start | bytes 6291456
  205.8 13.5 %collective-permute-start.1 = (f32[1024,8,256]{2,0,1:T(8,128)}, f32[1024,8,256]{2,0,1:T(8,128)S(1)}, u32[]{:S(2)}, u32[]{:S(2)}) collective-permute-start(f32[1024,8,256]{2,0,1:T(8,128)} %select_bitcast_fusion), channel_id=1, source_target_pairs={{0,1},{1,0},{2,3},{3,2},{4,5},{5,4},{6,7},{7,6},{8,9},{9,8},{10,11... | collective-permute-start | bytes 25165832 | tf_op jit(solution)/shard_map/ppermute | solution.py:32
  229.3 117.4 %copy-start.1 = (f32[256,2]{0,1:T(2,128)S(1)}, f32[256,2]{0,1:T(2,128)}, u32[]{:S(2)}) copy-start(f32[256,2]{0,1:T(2,128)} %param.10) | copy-start | bytes 6148
  229.3 134.0 %copy-start = (bf16[256,256]{1,0:T(8,128)(2,1)S(1)}, bf16[256,256]{1,0:T(8,128)(2,1)}, u32[]{:S(2)}) copy-start(bf16[256,256]{1,0:T(8,128)(2,1)} %param.7) | copy-start | bytes 393220
  342.1 18.6 %all-to-all-start.1 = ((f32[8,128,256]{2,1,0:T(8,128)}), f32[8,128,256]{2,1,0:T(8,128)S(1)}, u32[]{:S(2)}, u32[]{:S(2)}) async-start(f32[8,128,256]{2,1,0:T(8,128)} %bitcast.65), calls=%async_computation.2 | async-start | bytes 2097152 | tf_op jit(solution)/shard_map/all_to_all | solution.py:67
Sparse Core Ops, SparseCore 0:
  65.6 66.8 all-gather.1
  229.5 112.5 reduce-scatter.1
where the time goes:
time: 372 us; the launch traced here: 371 us
  waiting for transfers between devices  206 us (55%)
  blocking collectives  52 us (14%)
  matrix products  39.2 us (11%)
  other arithmetic  32.7 us (9%)
  local copies, waits for them, and re-layouts  21.9 us (6%)
  between operations  13.6 us (4%)
  starting transfers between devices  4.98 us (1%)
    reduce_scatter x1, waiting for transfers between devices, body(): shares = lax.psum_scatter(summed, 'chip', scatter_dimension=1, tiled=True)  113 us
    all_gather x1, waiting for transfers between devices, body(): mine = lax.all_gather(arrived, 'chip', axis=0, tiled=False)  67 us
    psum x1, blocking collectives, body(): squares = lax.psum(jnp.sum(values * values, axis=-1, keepdims=True), COL)  38.1 us
    all_to_all x1, blocking collectives, body(): lax.all_to_all(packed, 'row', split_axis=0, concat_axis=0, tiled=True)  13.9 us
    dot_general x1, matrix products, body(): outputs = jnp.dot(hidden, w_down[0], preferred_element_type=jnp.float32)  13.8 us
    all_to_all x1, waiting for transfers between devices, body(): lax.all_to_all(shares, 'row', split_axis=0, concat_axis=0, tiled=True)  13.7 us
    dot_general x1, matrix products, body(): up_part = jnp.dot(widened, w_up[0], preferred_element_type=jnp.float32)  13 us
    ppermute x2, waiting for transfers between devices, swap_cores(): return lax.ppermute(value, 'core', perm=[(0, 1), (1, 0)])  13 us
  transfers between devices with their start and end apart: 5, of which 4 were waited for; matrix products, arithmetic and copies ran while one was open for 3% of the time, Pallas kernels for 0%

commit v1 on v0

--- a/solution.py
+++ b/solution.py
@@ -38,7 +38,7 @@
     core = lax.axis_index("core")
     block = lax.axis_index("chip") * 2 + core
     values = tokens.astype(jnp.float32)
-    squares = lax.psum(jnp.sum(values * values, axis=-1, keepdims=True), COL)
+    squares = lax.psum(lax.psum(jnp.sum(values * values, axis=-1, keepdims=True), "core"), "chip")
     inverse_norm = lax.rsqrt(squares / (width * chips * 2) + 1e-05)
     gain = lax.dynamic_slice_in_dim(norm_gain, block * width, width)
     normed = (values * inverse_norm * gain).astype(jnp.bfloat16)

time: 372 us -> 360 us (0.968)
  blocking collectives: 52 us -> 40.8 us
    psum x1 -> x2, blocking collectives: 38.1 us -> 27 us  [the longest x1 24.5 us: body(): lax.psum(lax.psum(jnp.sum(values * values, axis=-1, keepdims=True), 'core...]
where the time goes in v1:
time: 360 us
  waiting for transfers between devices  206 us (57%)
  blocking collectives  40.8 us (11%)
  matrix products  39.2 us (11%)
  other arithmetic  32.7 us (9%)
  local copies, waits for them, and re-layouts  21.9 us (6%)
  between operations  13.6 us (4%)
  starting transfers between devices  4.98 us (1%)
    reduce_scatter x1, waiting for transfers between devices, body(): shares = lax.psum_scatter(summed, 'chip', scatter_dimension=1, tiled=True)  113 us
    all_gather x1, waiting for transfers between devices, body(): mine = lax.all_gather(arrived, 'chip', axis=0, tiled=False)  67 us
    psum x1, blocking collectives, body(): lax.psum(lax.psum(jnp.sum(values * values, axis=-1, keepdims=True), 'core...  24.5 us
    all_to_all x1, blocking collectives, body(): lax.all_to_all(packed, 'row', split_axis=0, concat_axis=0, tiled=True)  13.9 us
    dot_general x1, matrix products, body(): outputs = jnp.dot(hidden, w_down[0], preferred_element_type=jnp.float32)  13.8 us
    all_to_all x1, waiting for transfers between devices, body(): lax.all_to_all(shares, 'row', split_axis=0, concat_axis=0, tiled=True)  13.7 us
    dot_general x1, matrix products, body(): up_part = jnp.dot(widened, w_up[0], preferred_element_type=jnp.float32)  13 us
    ppermute x2, waiting for transfers between devices, swap_cores(): return lax.ppermute(value, 'core', perm=[(0, 1), (1, 0)])  13 us
  transfers between devices with their start and end apart: 5, of which 4 were waited for; matrix products, arithmetic and copies ran while one was open for 3% of the time, Pallas kernels for 0%

profile of v1, /device:TPU:0, one launch (start us, length us, event | category | flops | bytes accessed | tf_op | source)
XLA Modules:
  0.0 359.7 jit_solution(14562715813988002859)
XLA Ops:
  6.5 0.8 copy.51
  7.4 0.1 eq.48
  7.7 1.1 reduce-window.6
  8.8 0.2 slice_reduce_fusion
  9.2 0.1 reduce_sum.39
  9.4 0.7 compare_select_fusion
  10.1 0.3 convert_reduce_fusion
  10.4 1.0 fusion.9
  11.4 2.5 psum.14
  13.8 24.5 %psum.15 = f32[256,1]{0,1:T(1,128)S(1)} all-reduce(f32[256,1]{0,1:T(1,128)S(1)} %psum.14), channel_id=1, replica_groups=mesh['row'=8,'chip'=8,'core'=2] {'chip'}, use_global_device_ids=true, to_apply=%region_6.7 | all-reduce | flops 256 | bytes 2048 | tf_op jit(solution)/shard_map/psum | solution.py:41
  38.3 0.8 dynamic_slice.3
  39.1 1.3 convolution_convert_fusion
  40.4 13.9 %all_to_all.10 = bf16[8,128,256]{2,1,0:T(8,128)(2,1)} all-to-all(bf16[8,128,256]{2,1,0:T(8,128)(2,1)S(1)} %bitcast.66), channel_id=1, replica_groups=mesh['row'=8,'chip'=8,'core'=2] {'row'}, dimensions={0} | all-to-all | bytes 1048576 | tf_op jit(solution)/shard_map/all_to_all | solution.py:50
  54.4 67.0 %all-gather.2.cloned.1.call-done = bf16[8,1024,256]{2,1,0:T(8,128)(2,1)} async-done(((bf16[1,1024,256]{2,1,0:T(8,128)(2,1)}), bf16[8,1024,256]{2,1,0:T(8,128)(2,1)}) %all-gather.2.cloned.1.call-update) | async-done | bytes 4194320 | tf_op jit(solution)/shard_map/all_gather | solution.py:52
  121.4 6.4 %copy.54 = bf16[8,1024,256]{1,2,0:T(8,128)(2,1)} copy(bf16[8,1024,256]{2,1,0:T(8,128)(2,1)} %all-gather.2.cloned.1.call-done) | data formatting | bytes 8388608 | tf_op jit(solution)/shard_map/all_gather | solution.py:52
  127.8 10.8 %copy.64 = bf16[4096,896]{1,0:T(8,128)(2,1)} copy(bf16[4096,896]{0,1:T(8,128)(2,1)} %bitcast.60) | data formatting | bytes 14680064 | tf_op jit(solution)/shard_map/dot_general | solution.py:60
  138.7 7.9 %maximum_select_fusion = bf16[8,2,1024,256]{2,3,1,0:T(8,128)(2,1)S(1)} fusion(bf16[8,1,1024,256]{2,3,1,0:T(8,128)(2,1)} %bitcast.7, bf16[8,1,1024,256]{2,3,1,0:T(8,128)(2,1)} %bitcast.57, pred[]{:T(512)S(6)} %eq.43), kind=kLoop, calls=%fused_computation.1 | loop fusion | flops 12582912 | bytes 16777216 | tf_op jit(solution)/shard_map/jit(_where)/select_n | solution.py:54
  146.6 13.0 %fusion.2 = f32[1024,896]{1,0:T(8,128)S(1)} fusion(bf16[1024,4096]{0,1:T(8,128)(2,1)S(1)} %bitcast.58, bf16[1,4096,896]{2,1,0:T(8,128)(2,1)} %param.12), kind=kOutput, calls=%fused_computation.6 | convolution fusion | flops 7516192768 | bytes 19398656 | tf_op jit(solution)/shard_map/dot_general | solution.py:58
  159.7 11.1 %fusion.4 = f32[1024,896]{1,0:T(8,128)} fusion(bf16[1024,4096]{0,1:T(8,128)(2,1)S(1)} %bitcast.59, bf16[1,4096,896]{2,1,0:T(8,128)(2,1)S(1)} %bitcast.70), kind=kOutput, calls=%fused_computation.8 | convolution fusion | flops 7516192768 | bytes 19398656 | tf_op jit(solution)/shard_map/dot_general | solution.py:57
  170.8 13.8 %fusion.6 = f32[1024,8,2,256]{3,0,2,1:T(8,128)} fusion(bf16[8,2,256,896]{3,2,1,0:T(8,128)(2,1)S(1)} %bitcast.63, f32[1024,896]{1,0:T(8,128)S(1)} %fusion.2, f32[1024,896]{1,0:T(8,128)} %fusion.4), kind=kOutput, calls=%fused_computation.13 | convolution fusion | flops 7521697792 | bytes 31457280 | tf_op jit(solution)/shard_map/dot_general | solution.py:60
  184.6 10.1 %select_bitcast_fusion = f32[1024,8,256]{2,0,1:T(8,128)} fusion(f32[1024,8,2,256]{3,0,2,1:T(8,128)} %fusion.6, pred[]{:T(512)S(6)} %eq.43), kind=kLoop, calls=%fused_computation.5 | loop fusion | flops 2097152 | bytes 25165824 | tf_op jit(solution)/shard_map/jit(_where)/select_n | solution.py:63
  194.6 0.5 collective-permute-start.1
  195.2 13.0 %collective-permute-done.1 = f32[1024,8,256]{2,0,1:T(8,128)S(1)} collective-permute-done((f32[1024,8,256]{2,0,1:T(8,128)}, f32[1024,8,256]{2,0,1:T(8,128)S(1)}, u32[]{:S(2)}, u32[]{:S(2)}) %collective-permute-start.1) | collective-permute-done | bytes 8388640 | tf_op jit(solution)/shard_map/ppermute | solution.py:32
  208.2 10.0 %fusion.1 = f32[1024,8,256]{2,0,1:T(8,128)} fusion(f32[1024,8,256]{2,0,1:T(8,128)S(1)} %collective-permute-done.1, f32[1024,8,2,256]{3,0,2,1:T(8,128)} %fusion.6, pred[]{:T(512)S(6)} %eq.43), kind=kLoop, calls=%fused_computation.4 | loop fusion | flops 4194304 | bytes 33554432 | tf_op jit(solution)/shard_map/add | solution.py:64
  218.2 112.7 %reduce-scatter.2.cloned.1.call-done = f32[1024,1,256]{2,0,1:T(8,128)} async-done(((f32[1024,8,256]{2,0,1:T(8,128)}), f32[1024,1,256]{2,0,1:T(8,128)}) %reduce-scatter.2.cloned.1.call-update) | async-done | bytes 1048592 | tf_op jit(solution)/shard_map/reduce_scatter | solution.py:65
  330.9 4.4 %all-to-all-start.1 = ((f32[8,128,256]{2,1,0:T(8,128)}), f32[8,128,256]{2,1,0:T(8,128)S(1)}, u32[]{:S(2)}, u32[]{:S(2)}) async-start(f32[8,128,256]{2,1,0:T(8,128)} %bitcast.65), calls=%async_computation.2 | async-start | bytes 2097152 | tf_op jit(solution)/shard_map/all_to_all | solution.py:67
  335.5 0.1 reshape.53
  335.8 13.7 %all-to-all-done.1 = f32[8,128,256]{2,1,0:T(8,128)S(1)} async-done(((f32[8,128,256]{2,1,0:T(8,128)}), f32[8,128,256]{2,1,0:T(8,128)S(1)}, u32[]{:S(2)}, u32[]{:S(2)}) %all-to-all-start.1) | async-done | bytes 1048608 | tf_op jit(solution)/shard_map/all_to_all | solution.py:67
  349.5 1.6 gather_fusion
  351.1 0.3 reshape.52
  351.4 0.7 multiply_reduce_fusion
  352.1 0.7 fusion.12
  (30 shorter events, 0.7 us)
Async XLA Ops:
  6.5 114.8 %all-gather.2.cloned.1.call-start = ((), (), s32[]{:S(2)}) async-start(), calls=%async_computation.3 | async-start | bytes 4718592 | tf_op jit(solution)/shard_map/all_gather | solution.py:52
  54.3 276.6 %reduce-scatter.2.cloned.1.call-start = ((), (), s32[]{:S(2)}) async-start(), calls=%async_computation.4 | async-start | bytes 9437184 | tf_op jit(solution)/shard_map/reduce_scatter | solution.py:65
  127.8 10.8 %collective-permute-start = (bf16[8,1024,256]{1,2,0:T(8,128)(2,1)}, bf16[8,1024,256]{1,2,0:T(8,128)(2,1)}, u32[]{:S(2)}, u32[]{:S(2)}) collective-permute-start(bf16[8,1024,256]{1,2,0:T(8,128)(2,1)} %copy.54), channel_id=1, source_target_pairs={{0,1},{1,0},{2,3},{3,2},{4,5},{5,4},{6,7},{7,6},{8,9},{9,8},{10,11... | collective-permute-start | bytes 12582920 | tf_op jit(solution)/shard_map/ppermute | solution.py:32
  138.7 21.0 %slice-start.2 = ((s8[7340032]{0:T(1024)(128)(4,1)}), s8[4194304]{0:T(1024)(128)(4,1)S(1)}, s32[]{:S(2)}) async-start(s8[7340032]{0:T(1024)(128)(4,1)} %bitcast.69), calls=%async_computation.7 | async-start | bytes 8388608
  146.6 13.1 %slice-start.3 = ((s8[7340032]{0:T(1024)(128)(4,1)}), s8[3145728]{0:T(1024)(128)(4,1)S(1)}, s32[]{:S(2)}) async-start(s8[7340032]{0:T(1024)(128)(4,1)} %bitcast.69), calls=%async_computation.8 | async-start | bytes 6291456
  146.6 24.2 %slice-start = ((s8[7340032]{0:T(1024)(128)(4,1)}), s8[4194304]{0:T(1024)(128)(4,1)S(1)}, s32[]{:S(2)}) async-start(s8[7340032]{0:T(1024)(128)(4,1)} %bitcast.61), calls=%async_computation.5 | async-start | bytes 8388608
  159.7 11.1 %slice-start.1 = ((s8[7340032]{0:T(1024)(128)(4,1)}), s8[3145728]{0:T(1024)(128)(4,1)S(1)}, s32[]{:S(2)}) async-start(s8[7340032]{0:T(1024)(128)(4,1)} %bitcast.61), calls=%async_computation.6 | async-start | bytes 6291456
  194.6 13.5 %collective-permute-start.1 = (f32[1024,8,256]{2,0,1:T(8,128)}, f32[1024,8,256]{2,0,1:T(8,128)S(1)}, u32[]{:S(2)}, u32[]{:S(2)}) collective-permute-start(f32[1024,8,256]{2,0,1:T(8,128)} %select_bitcast_fusion), channel_id=1, source_target_pairs={{0,1},{1,0},{2,3},{3,2},{4,5},{5,4},{6,7},{7,6},{8,9},{9,8},{10,11... | collective-permute-start | bytes 25165832 | tf_op jit(solution)/shard_map/ppermute | solution.py:32
  218.2 117.4 %copy-start.1 = (f32[256,2]{0,1:T(2,128)S(1)}, f32[256,2]{0,1:T(2,128)}, u32[]{:S(2)}) copy-start(f32[256,2]{0,1:T(2,128)} %param.10) | copy-start | bytes 6148
  218.2 134.0 %copy-start = (bf16[256,256]{1,0:T(8,128)(2,1)S(1)}, bf16[256,256]{1,0:T(8,128)(2,1)}, u32[]{:S(2)}) copy-start(bf16[256,256]{1,0:T(8,128)(2,1)} %param.7) | copy-start | bytes 393220
  330.9 18.6 %all-to-all-start.1 = ((f32[8,128,256]{2,1,0:T(8,128)}), f32[8,128,256]{2,1,0:T(8,128)S(1)}, u32[]{:S(2)}, u32[]{:S(2)}) async-start(f32[8,128,256]{2,1,0:T(8,128)} %bitcast.65), calls=%async_computation.2 | async-start | bytes 2097152 | tf_op jit(solution)/shard_map/all_to_all | solution.py:67
Sparse Core Ops, SparseCore 0:
  54.4 66.8 all-gather.1
  218.3 112.5 reduce-scatter.1
